TPU v7x, 512 devices: a whole 4x4x16 slice. The times are simulated.
512 devices in a mesh: lev: 16 (over x, z_hi, core), hor: 32 (over z_lo, y).
Axes of the slice: x: 4, y: 4, z: 16 (z_hi: 2, z_lo: 8; z = z_hi * 8 + z_lo), core: 2. Of those that a mesh axis runs over, the one named last changes fastest.
Arguments:
- state: float32 [2, 128, 512, 1024], P(None, 'lev', 'hor'), may hold values from -6 to 6
- cotangent: bfloat16 [2, 128, 512, 1024], P(None, 'lev', 'hor'), may hold values from -6 to 6
- diffusion: float32 [128, 512, 1024], P('lev', 'hor'), may hold values from 0.02 to 0.2
- vertical_inverse: float32 [2, 128, 128], replicated, may hold values from -0.2 to 2
- w_in: bfloat16 [1024, 256], replicated, may hold values from -0.375 to 0.375
- w_out: bfloat16 [256, 1024], replicated, may hold values from -0.1875 to 0.1875
Outputs:
- state_adjoint: float32 [2, 128, 512, 1024], P(None, 'lev', 'hor')
All inputs are finite; a program needn't handle non-finite values.
Results may differ from a plain program's by a relative error of at most 0.002.
Values may be sent and summed in bfloat16 or wider, within the bound.
A program may use at most 64 MiB of HBM per device.

v0:
```python
import jax
import jax.numpy as jnp
from jax import lax
from jax.sharding import PartitionSpec as P


def with_halo(block, sides, width):
    for axis, dim in sides:
        count = lax.axis_size(axis)
        forward = [(i, i + 1) for i in range(count - 1)]
        backward = [(target, source) for source, target in forward]
        low = lax.ppermute(
            lax.slice_in_dim(block, block.shape[dim] - width, None, axis=dim), axis, forward
        )
        high = lax.ppermute(lax.slice_in_dim(block, 0, width, axis=dim), axis, backward)
        block = jnp.concatenate([low, block, high], axis=dim)
    return block


def laplace_local(extended):
    padded = jnp.pad(extended, ((0, 0), (0, 0), (0, 0), (1, 1)))
    return (
        padded[:, :, 2:, 1:-1]
        + padded[:, :, :-2, 1:-1]
        + padded[:, :, 1:-1, 2:]
        + padded[:, :, 1:-1, :-2]
        - 4.0 * padded[:, :, 1:-1, 1:-1]
    )


def column_adjoint(diffused, cot_block, vertical_inverse, w_in, w_out):
    highest = lax.Precision.HIGHEST
    solved = jnp.einsum("fkl,flc->fkc", vertical_inverse, diffused, precision=highest)
    fields, levels, count = solved.shape
    inputs = solved.reshape(fields * levels, count).astype(jnp.bfloat16)
    preact = jnp.dot(w_in, inputs, preferred_element_type=jnp.float32)
    cot_cols = cot_block.reshape(fields * levels, count)
    hidden_grad = lax.dot_general(
        w_out, cot_cols, (((0,), (0,)), ((), ())), preferred_element_type=jnp.float32
    )
    squashed = jax.nn.sigmoid(preact)
    pre_grad = (hidden_grad * squashed * (1.0 + preact * (1.0 - squashed))).astype(jnp.bfloat16)
    level_grad = cot_cols.astype(jnp.float32) + lax.dot_general(
        w_in, pre_grad, (((0,), (0,)), ((), ())), preferred_element_type=jnp.float32
    )
    level_grad = level_grad.reshape(fields, levels, count)
    return jnp.einsum("fkl,fkc->flc", vertical_inverse, level_grad, precision=highest)


def body(state, cotangent, diffusion, vertical_inverse, w_in, w_out):
    extended = with_halo(state, (("hor", 2),), 1)
    diffused = state + diffusion[None] * laplace_local(extended)
    state_cols = lax.all_to_all(diffused, "lev", split_axis=3, concat_axis=1, tiled=True)
    cot_cols = lax.all_to_all(cotangent, "lev", split_axis=3, concat_axis=1, tiled=True)
    shape_cols = state_cols.shape
    flat_state = state_cols.reshape(shape_cols[0], shape_cols[1], shape_cols[2] * shape_cols[3])
    flat_cot = cot_cols.reshape(shape_cols[0], shape_cols[1], shape_cols[2] * shape_cols[3])
    adjoint_cols = column_adjoint(flat_state, flat_cot, vertical_inverse, w_in, w_out).reshape(
        shape_cols
    )
    adjoint_levels = lax.all_to_all(adjoint_cols, "lev", split_axis=1, concat_axis=3, tiled=True)
    weighted = diffusion[None] * adjoint_levels
    rimmed = with_halo(weighted, (("hor", 2),), 1)
    return adjoint_levels + laplace_local(rimmed)


def solution(mesh):
    placed = (
        P(None, "lev", "hor", None),
        P(None, "lev", "hor", None),
        P("lev", "hor", None),
        P(),
        P(),
        P(),
    )
    return jax.shard_map(
        body, mesh=mesh, in_specs=placed, out_specs=P(None, "lev", "hor", None), check_vma=False
    )
```

profile of v0, /device:TPU:32, one launch (start us, length us, event | category | flops | bytes accessed | tf_op | source)
XLA Modules:
  0.0 259.4 jit_solution(9660499994656659942)
XLA Ops:
  0.0 5.8 %copy.21 = bf16[2,8,16,1024]{2,1,0,3:T(8,128)(2,1)} copy(bf16[2,8,16,1024]{3,2,1,0:T(8,128)(2,1)} %param.7) | data formatting | bytes 1048576 | tf_op args[1]
  5.8 6.5 %reshape.19 = bf16[16,2,8192]{2,1,0:T(2,128)(2,1)} reshape(bf16[1024,2,8,16]{3,2,1,0:T(8,128)(2,1)} %bitcast.61) | data formatting | bytes 1048576
  12.3 16.8 %all-to-all-start = ((bf16[16,2,8192]{2,1,0:T(2,128)(2,1)}), bf16[16,2,8192]{2,1,0:T(2,128)(2,1)}, u32[]{:S(2)}, u32[]{:S(2)}) async-start(bf16[16,2,8192]{2,1,0:T(2,128)(2,1)} %reshape.19), calls=%async_computation | async-start | bytes 1048576 | tf_op jit(solution)/shard_map/all_to_all | solution.py:54
  29.1 0.0 copy-start.2
  29.1 0.1 fusion.17
  29.2 5.5 %collective-permute-start = (f32[2,8,1,1024]{3,2,1,0:T(1,128)S(1)}, f32[2,8,1,1024]{3,2,1,0:T(1,128)S(1)}, u32[]{:S(2)}, u32[]{:S(2)}) collective-permute-start(f32[2,8,1,1024]{3,2,1,0:T(1,128)S(1)} %get-tuple-element.8), channel_id=1, source_target_pairs={{1,0},{2,1},{3,2},{4,3},{5,4},{6,5},{7,6},{8,7},{9,8},{10,9},{11,1... | collective-permute-start | bytes 196616 | tf_op jit(solution)/shard_map/ppermute | solution.py:15
  34.7 1.9 collective-permute-start.1
  36.7 17.3 %collective-permute-done = f32[2,8,1,1024]{3,2,1,0:T(1,128)S(1)} collective-permute-done((f32[2,8,1,1024]{3,2,1,0:T(1,128)S(1)}, f32[2,8,1,1024]{3,2,1,0:T(1,128)S(1)}, u32[]{:S(2)}, u32[]{:S(2)}) %collective-permute-start) | collective-permute-done | bytes 65568 | tf_op jit(solution)/shard_map/ppermute | solution.py:15
  53.9 0.0 collective-permute-done.1
  53.9 0.9 select_maximum_fusion.2
  54.9 0.7 fusion.13
  55.6 6.1 %copy.23 = f32[2,8,16,1024]{2,1,0,3:T(8,128)} copy(f32[2,8,16,1024]{3,2,1,0:T(8,128)S(1)} %fusion.13) | data formatting | bytes 2097152 | tf_op jit(solution)/shard_map/add | solution.py:52
  61.7 7.1 %reshape.17 = f32[16,1,16384]{2,1,0:T(1,128)} reshape(f32[1024,2,8,16]{3,2,1,0:T(8,128)} %bitcast.59) | data formatting | bytes 2097152
  68.9 0.0 all-to-all-done
  68.9 14.2 %all-to-all-start.1 = ((f32[16,1,16384]{2,1,0:T(1,128)}), f32[16,1,16384]{2,1,0:T(1,128)S(1)}, u32[]{:S(2)}, u32[]{:S(2)}) async-start(f32[16,1,16384]{2,1,0:T(1,128)} %reshape.17), calls=%async_computation.1 | async-start | bytes 2097152 | tf_op jit(solution)/shard_map/all_to_all | solution.py:53
  83.0 5.4 %reshape.20 = bf16[1024,2,8,16]{3,2,1,0:T(8,128)(2,1)} reshape(bf16[16,2,8192]{2,1,0:T(2,128)(2,1)} %all-to-all-done) | data formatting | bytes 1048576
  88.4 4.0 %copy.22 = bf16[2,8,16,16,64]{4,2,1,3,0:T(8,128)(2,1)S(1)} copy(bf16[2,8,16,16,64]{2,1,0,4,3:T(8,128)(2,1)} %bitcast.60) | data formatting | bytes 1048576 | tf_op jit(solution)/shard_map/all_to_all | solution.py:54
  92.4 1.6 reshape_reshape.3
  94.0 45.7 %all-to-all-done.1 = f32[16,1,16384]{2,1,0:T(1,128)S(1)} async-done(((f32[16,1,16384]{2,1,0:T(1,128)}), f32[16,1,16384]{2,1,0:T(1,128)S(1)}, u32[]{:S(2)}, u32[]{:S(2)}) %all-to-all-start.1) | async-done | bytes 1048608 | tf_op jit(solution)/shard_map/all_to_all | solution.py:53
  139.7 0.6 broadcast.42
  140.3 3.1 %reduce = f32[16,16384]{1,0:T(8,128)S(1)} reduce(f32[16,1,16384]{2,1,0:T(1,128)S(1)} %all-to-all-done.1, f32[]{:T(128)} %broadcast.42), dimensions={1}, to_apply=%all_to_all.38.reduce_sub_computation | reduce | bytes 2097156 | tf_op jit(solution)/shard_map/all_to_all | solution.py:53
  143.4 4.8 %reshape.18 = f32[1024,2,8,16]{3,2,1,0:T(8,128)} reshape(f32[16,16384]{1,0:T(8,128)S(1)} %reduce) | data formatting | bytes 2097152
  148.2 5.4 %copy.24 = f32[2,8,16,16,64]{4,2,1,3,0:T(8,128)S(1)} copy(f32[2,8,16,16,64]{2,1,0,4,3:T(8,128)} %bitcast.58) | data formatting | bytes 2097152 | tf_op jit(solution)/shard_map/all_to_all | solution.py:53
  153.6 0.0 copy-start.4
  153.6 1.5 reshape.14
  155.2 2.3 convolution_convert_fusion
  157.4 0.0 copy-done
  157.4 0.0 copy-start.3
  157.5 0.0 copy-start.5
  157.5 2.7 %fusion.19 = f32[1024,1024]{0,1:T(8,128)} fusion(bf16[1024,256]{1,0:T(8,128)(2,1)S(1)} %copy-done, bf16[256,1024]{1,0:T(8,128)(2,1)S(1)} %bitcast.67), kind=kOutput, calls=%fused_computation.38 | convolution fusion | flops 536870912 | bytes 5242880 | tf_op jit(solution)/shard_map/dot_general | solution.py:36
  160.1 0.0 copy-done.5
  160.1 4.4 %fusion.7 = f32[256,1024]{1,0:T(8,128)S(1)} fusion(bf16[1024,256]{1,0:T(8,128)(2,1)S(1)} %copy-done, f32[1024,1024]{0,1:T(8,128)} %fusion.19, bf16[256,1024]{1,0:T(8,128)(2,1)S(1)} %copy-done.5, bf16[256,1024]{1,0:T(8,128)(2,1)S(1)} %copy-done.3), kind=kOutput, calls=%fused_computation.16 | convolution fusion | flops 1083703296 | bytes 6815744 | tf_op jit(solution)/shard_map/dot_general | solution.py:43
  164.6 2.8 %fusion.18 = f32[2,1024,128]{2,1,0:T(8,128)} fusion(f32[2,128,1024]{2,1,0:T(8,128)S(1)} %bitcast.68, f32[2,128,128]{2,1,0:T(8,128)S(1)} %copy-done.4), kind=kOutput, calls=%fused_computation.37 | convolution fusion | flops 402653184 | bytes 2228224 | tf_op jit(solution)/shard_map/fkl,fkc->flc/dot_general | solution.py:47
  167.3 3.1 %copy.27 = f32[2,128,16,64]{3,2,0,1:T(8,128)S(1)} copy(f32[2,128,16,64]{1,3,2,0:T(8,128)} %bitcast.66) | data formatting | bytes 2097152 | tf_op jit(solution)/shard_map/reshape | solution.py:58
  170.4 2.3 reshape.21
  172.7 62.7 %all_to_all.48 = f32[16,1,16384]{2,1,0:T(1,128)S(1)} all-to-all(f32[16,1,16384]{2,1,0:T(1,128)} %reshape.21), channel_id=1, replica_groups=mesh['lev'=16,'hor'=32] {'lev'}, dimensions={0} | all-to-all | bytes 2097152 | tf_op jit(solution)/shard_map/all_to_all | solution.py:61
  235.4 4.4 %reduce.1 = f32[16,16384]{1,0:T(8,128)} reduce(f32[16,1,16384]{2,1,0:T(1,128)S(1)} %all_to_all.48, f32[]{:T(128)} %broadcast.42), dimensions={1}, to_apply=%all_to_all.41.reduce_sub_computation | reduce | bytes 2097156 | tf_op jit(solution)/shard_map/all_to_all | solution.py:61
  239.7 2.1 reshape.22
  241.8 2.6 copy.29
  244.3 2.0 all_to_all.44
  246.4 0.1 broadcast_multiply_fusion
  246.5 0.1 fusion.16
  246.6 1.9 collective-permute-start.2
  248.5 3.9 %collective-permute-start.3 = (f32[2,8,1,1024]{3,2,1,0:T(1,128)S(1)}, f32[2,8,1,1024]{3,2,1,0:T(1,128)S(1)}, u32[]{:S(2)}, u32[]{:S(2)}) collective-permute-start(f32[2,8,1,1024]{3,2,1,0:T(1,128)S(1)} %get-tuple-element.5), channel_id=1, source_target_pairs={{0,1},{1,2},{2,3},{3,4},{4,5},{5,6},{6,7},{7,8},{8,9},{9,10},{10,1... | collective-permute-start | bytes 196616 | tf_op jit(solution)/shard_map/ppermute | solution.py:12
  252.4 0.3 collective-permute-done.2
  252.7 4.0 %collective-permute-done.3 = f32[2,8,1,1024]{3,2,1,0:T(1,128)S(1)} collective-permute-done((f32[2,8,1,1024]{3,2,1,0:T(1,128)S(1)}, f32[2,8,1,1024]{3,2,1,0:T(1,128)S(1)}, u32[]{:S(2)}, u32[]{:S(2)}) %collective-permute-start.3) | collective-permute-done | bytes 65568 | tf_op jit(solution)/shard_map/ppermute | solution.py:12
  256.8 0.9 select_maximum_fusion
  257.7 1.7 fusion.9
  (6 shorter events, 0.0 us)
Async XLA Ops:
  0.0 157.4 %copy-start = (bf16[1024,256]{1,0:T(8,128)(2,1)S(1)}, bf16[1024,256]{1,0:T(8,128)(2,1)}, u32[]{:S(2)}) copy-start(bf16[1024,256]{1,0:T(8,128)(2,1)} %param.10) | copy-start | bytes 1572868
  5.8 23.3 %copy-start.1 = (f32[2,8,16,1024]{3,2,1,0:T(8,128)S(1)}, f32[2,8,16,1024]{3,2,1,0:T(8,128)}, u32[]{:S(2)}) copy-start(f32[2,8,16,1024]{3,2,1,0:T(8,128)} %param.6) | copy-start | bytes 3145732
  12.3 56.6 %all-to-all-start = ((bf16[16,2,8192]{2,1,0:T(2,128)(2,1)}), bf16[16,2,8192]{2,1,0:T(2,128)(2,1)}, u32[]{:S(2)}, u32[]{:S(2)}) async-start(bf16[16,2,8192]{2,1,0:T(2,128)(2,1)} %reshape.19), calls=%async_computation | async-start | bytes 1048576 | tf_op jit(solution)/shard_map/all_to_all | solution.py:54
  29.1 25.7 %copy-start.2 = (f32[8,16,1024]{2,1,0:T(8,128)S(1)}, f32[8,16,1024]{2,1,0:T(8,128)}, u32[]{:S(2)}) copy-start(f32[8,16,1024]{2,1,0:T(8,128)} %param.8) | copy-start | bytes 1572868
  29.2 24.7 %collective-permute-start = (f32[2,8,1,1024]{3,2,1,0:T(1,128)S(1)}, f32[2,8,1,1024]{3,2,1,0:T(1,128)S(1)}, u32[]{:S(2)}, u32[]{:S(2)}) collective-permute-start(f32[2,8,1,1024]{3,2,1,0:T(1,128)S(1)} %get-tuple-element.8), channel_id=1, source_target_pairs={{1,0},{2,1},{3,2},{4,3},{5,4},{6,5},{7,6},{8,7},{9,8},{10,9},{11,1... | collective-permute-start | bytes 196616 | tf_op jit(solution)/shard_map/ppermute | solution.py:15
  34.7 19.2 %collective-permute-start.1 = (f32[2,8,1,1024]{3,2,1,0:T(1,128)S(1)}, f32[2,8,1,1024]{3,2,1,0:T(1,128)S(1)}, u32[]{:S(2)}, u32[]{:S(2)}) collective-permute-start(f32[2,8,1,1024]{3,2,1,0:T(1,128)S(1)} %get-tuple-element.7), channel_id=1, source_target_pairs={{0,1},{1,2},{2,3},{3,4},{4,5},{5,6},{6,7},{7,8},{8,9},{9,10},{10,1... | collective-permute-start | bytes 196616 | tf_op jit(solution)/shard_map/ppermute | solution.py:12
  68.9 70.9 %all-to-all-start.1 = ((f32[16,1,16384]{2,1,0:T(1,128)}), f32[16,1,16384]{2,1,0:T(1,128)S(1)}, u32[]{:S(2)}, u32[]{:S(2)}) async-start(f32[16,1,16384]{2,1,0:T(1,128)} %reshape.17), calls=%async_computation.1 | async-start | bytes 2097152 | tf_op jit(solution)/shard_map/all_to_all | solution.py:53
  153.6 1.6 copy-start.4
  157.4 2.7 %copy-start.3 = (bf16[256,1024]{1,0:T(8,128)(2,1)S(1)}, bf16[256,1024]{1,0:T(8,128)(2,1)}, u32[]{:S(2)}) copy-start(bf16[256,1024]{1,0:T(8,128)(2,1)} %reshape_reshape.3) | copy-start | bytes 1572868
  157.5 2.7 %copy-start.5 = (bf16[256,1024]{1,0:T(8,128)(2,1)S(1)}, bf16[256,1024]{1,0:T(8,128)(2,1)}, u32[]{:S(2)}) copy-start(bf16[256,1024]{1,0:T(8,128)(2,1)} %param.11) | copy-start | bytes 1572868
  246.6 6.2 %collective-permute-start.2 = (f32[2,8,1,1024]{3,2,1,0:T(1,128)S(1)}, f32[2,8,1,1024]{3,2,1,0:T(1,128)S(1)}, u32[]{:S(2)}, u32[]{:S(2)}) collective-permute-start(f32[2,8,1,1024]{3,2,1,0:T(1,128)S(1)} %get-tuple-element.6), channel_id=1, source_target_pairs={{1,0},{2,1},{3,2},{4,3},{5,4},{6,5},{7,6},{8,7},{9,8},{10,9},{11,1... | collective-permute-start | bytes 196616 | tf_op jit(solution)/shard_map/ppermute | solution.py:15
  248.5 8.3 %collective-permute-start.3 = (f32[2,8,1,1024]{3,2,1,0:T(1,128)S(1)}, f32[2,8,1,1024]{3,2,1,0:T(1,128)S(1)}, u32[]{:S(2)}, u32[]{:S(2)}) collective-permute-start(f32[2,8,1,1024]{3,2,1,0:T(1,128)S(1)} %get-tuple-element.5), channel_id=1, source_target_pairs={{0,1},{1,2},{2,3},{3,4},{4,5},{5,6},{6,7},{7,8},{8,9},{9,10},{10,1... | collective-permute-start | bytes 196616 | tf_op jit(solution)/shard_map/ppermute | solution.py:12
where the time goes:
time: 260 us; the launch traced here: 259 us
  waiting for transfers between devices  67.3 us (26%)
  blocking collectives  62.7 us (24%)
  local copies, waits for them, and re-layouts  60.9 us (23%)
  starting transfers between devices  44.2 us (17%)
  matrix products  12.1 us (5%)
  other arithmetic  11.8 us (5%)
    all_to_all x1, blocking collectives, body(): lax.all_to_all(adjoint_cols, 'lev', split_axis=1, concat_axis=3, tiled=True)  62.7 us
    all_to_all x1, waiting for transfers between devices, body(): lax.all_to_all(diffused, 'lev', split_axis=3, concat_axis=1, tiled=True)  45.7 us
    unnamed x19, local copies, waits for them, and re-layouts  33.9 us
    ppermute x2, waiting for transfers between devices, with_halo(): lax.ppermute(lax.slice_in_dim(block, 0, width, axis=dim), axis, backward)  17.6 us
    all_to_all x1, starting transfers between devices, body(): lax.all_to_all(cotangent, 'lev', split_axis=3, concat_axis=1, tiled=True)  16.8 us
    all_to_all x1, starting transfers between devices, body(): lax.all_to_all(diffused, 'lev', split_axis=3, concat_axis=1, tiled=True)  14.2 us
    ppermute x2, starting transfers between devices, with_halo(): lax.ppermute(lax.slice_in_dim(block, 0, width, axis=dim), axis, backward)  7.42 us
    add x1, local copies, waits for them, and re-layouts, body(): diffused = state + diffusion[None] * laplace_local(extended)  6.14 us
  transfers between devices with their start and end apart: 6, of which 4 were waited for; matrix products, arithmetic and copies ran while one was open for 10% of the time, Pallas kernels for 0%

commit v1 on v0

--- a/solution.py
+++ b/solution.py
@@ -50,7 +50,10 @@
 def body(state, cotangent, diffusion, vertical_inverse, w_in, w_out):
     extended = with_halo(state, (("hor", 2),), 1)
     diffused = state + diffusion[None] * laplace_local(extended)
-    state_cols = lax.all_to_all(diffused, "lev", split_axis=3, concat_axis=1, tiled=True)
+    state_cols = jnp.concatenate(
+        lax.all_to_all(jnp.stack(jnp.split(diffused, lax.axis_size("lev"), axis=3)), "lev", 0, 0),
+        axis=1,
+    )
     cot_cols = lax.all_to_all(cotangent, "lev", split_axis=3, concat_axis=1, tiled=True)
     shape_cols = state_cols.shape
     flat_state = state_cols.reshape(shape_cols[0], shape_cols[1], shape_cols[2] * shape_cols[3])

time: 260 us -> 212 us (0.82)
  the two profiles are of different devices: /device:TPU:32 before, /device:TPU:24 now
where the time goes in v1:
time: 212 us; the launch traced here: 211 us
  starting transfers between devices  73.3 us (35%)
  local copies, waits for them, and re-layouts  46 us (22%)
  waiting for transfers between devices  35.7 us (17%)
  blocking collectives  32 us (15%)
  other arithmetic  12.9 us (6%)
  matrix products  11.1 us (5%)
    ppermute x2, starting transfers between devices, with_halo(): lax.ppermute(lax.slice_in_dim(block, block.shape[dim] - width, None, axis...  47.3 us
    all_to_all x1, blocking collectives, body(): lax.all_to_all(adjoint_cols, 'lev', split_axis=1, concat_axis=3, tiled=True)  32 us
    unnamed x32, local copies, waits for them, and re-layouts  27 us
    all_to_all x1, starting transfers between devices, body(): lax.all_to_all(cotangent, 'lev', split_axis=3, concat_axis=1, tiled=True)  17.8 us
    all_to_all x1, waiting for transfers between devices, body(): lax.all_to_all(cotangent, 'lev', split_axis=3, concat_axis=1, tiled=True)  15.1 us
    all_to_all x1, waiting for transfers between devices, body(): lax.all_to_all(jnp.stack(jnp.split(diffused, lax.axis_size('lev'), axis=3...  14.2 us
    ppermute x2, waiting for transfers between devices, with_halo(): lax.ppermute(lax.slice_in_dim(block, 0, width, axis=dim), axis, backward)  6.33 us
    dot_general x1, matrix products, column_adjoint(): lax.dot_general(w_in, pre_grad, (((0,), (0,)), ((), ())), preferred_eleme...  4.6 us
  transfers between devices with their start and end apart: 6, of which 3 were waited for; matrix products, arithmetic and copies ran while one was open for 13% of the time, Pallas kernels for 0%

profile of v1, /device:TPU:24, one launch (start us, length us, event | category | flops | bytes accessed | tf_op | source)
XLA Modules:
  0.0 211.3 jit_solution(12131683830835069768)
XLA Ops:
  0.0 1.4 fusion.33
  1.4 3.5 %collective-permute-start.1 = (f32[2,8,1,1024]{3,2,1,0:T(1,128)S(1)}, f32[2,8,1,1024]{3,2,1,0:T(1,128)S(1)}, u32[]{:S(2)}, u32[]{:S(2)}) collective-permute-start(f32[2,8,1,1024]{3,2,1,0:T(1,128)S(1)} %get-tuple-element.7), channel_id=1, source_target_pairs={{0,1},{1,2},{2,3},{3,4},{4,5},{5,6},{6,7},{7,8},{8,9},{9,10},{10,1... | collective-permute-start | bytes 196616 | tf_op jit(solution)/shard_map/ppermute | solution.py:12
  4.9 2.4 %collective-permute-start = (f32[2,8,1,1024]{3,2,1,0:T(1,128)S(1)}, f32[2,8,1,1024]{3,2,1,0:T(1,128)S(1)}, u32[]{:S(2)}, u32[]{:S(2)}) collective-permute-start(f32[2,8,1,1024]{3,2,1,0:T(1,128)S(1)} %get-tuple-element.8), channel_id=1, source_target_pairs={{1,0},{2,1},{3,2},{4,3},{5,4},{6,5},{7,6},{8,7},{9,8},{10,9},{11,1... | collective-permute-start | bytes 196616 | tf_op jit(solution)/shard_map/ppermute | solution.py:15
  7.2 5.7 %copy.21 = bf16[2,8,16,1024]{2,1,0,3:T(8,128)(2,1)} copy(bf16[2,8,16,1024]{3,2,1,0:T(8,128)(2,1)} %param.7) | data formatting | bytes 1048576 | tf_op args[1]
  12.9 6.5 %reshape.18 = bf16[16,2,8192]{2,1,0:T(2,128)(2,1)} reshape(bf16[1024,2,8,16]{3,2,1,0:T(8,128)(2,1)} %bitcast.120) | data formatting | bytes 1048576
  19.4 17.8 %all-to-all-start = ((bf16[16,2,8192]{2,1,0:T(2,128)(2,1)}), bf16[16,2,8192]{2,1,0:T(2,128)(2,1)}, u32[]{:S(2)}, u32[]{:S(2)}) async-start(bf16[16,2,8192]{2,1,0:T(2,128)(2,1)} %reshape.18), calls=%async_computation | async-start | bytes 1048576 | tf_op jit(solution)/shard_map/all_to_all | solution.py:57
  37.3 0.0 collective-permute-done.1
  37.3 0.9 select_maximum_fusion.2
  38.2 0.7 fusion.13
  39.0 0.1 fusion.29
  39.1 0.1 fusion.27
  39.2 0.1 fusion.25
  39.4 0.1 fusion.23
  39.5 0.1 fusion.21
  39.6 0.1 fusion.19
  39.7 0.1 fusion.17
  39.9 0.1 fusion.15
  40.0 2.3 %reshape.16 = f32[16,1,16384]{2,1,0:T(1,128)} reshape(f32[16,2,8,16,64]{4,3,2,1,0:T(8,128)S(1)} %fusion.15) | data formatting | bytes 2097152
  42.2 15.1 %all-to-all-done = bf16[16,2,8192]{2,1,0:T(2,128)(2,1)} async-done(((bf16[16,2,8192]{2,1,0:T(2,128)(2,1)}), bf16[16,2,8192]{2,1,0:T(2,128)(2,1)}, u32[]{:S(2)}, u32[]{:S(2)}) %all-to-all-start) | async-done | bytes 524320 | tf_op jit(solution)/shard_map/all_to_all | solution.py:57
  57.4 3.8 %all-to-all-start.1 = ((f32[16,1,16384]{2,1,0:T(1,128)}), f32[16,1,16384]{2,1,0:T(1,128)S(1)}, u32[]{:S(2)}, u32[]{:S(2)}) async-start(f32[16,1,16384]{2,1,0:T(1,128)} %reshape.16), calls=%async_computation.1 | async-start | bytes 2097152 | tf_op jit(solution)/shard_map/all_to_all | solution.py:54
  61.2 5.4 %reshape.19 = bf16[1024,2,8,16]{3,2,1,0:T(8,128)(2,1)} reshape(bf16[16,2,8192]{2,1,0:T(2,128)(2,1)} %all-to-all-done) | data formatting | bytes 1048576
  66.6 4.0 %copy.22 = bf16[2,8,16,16,64]{4,2,1,3,0:T(8,128)(2,1)S(1)} copy(bf16[2,8,16,16,64]{2,1,0,4,3:T(8,128)(2,1)} %bitcast.119) | data formatting | bytes 1048576 | tf_op jit(solution)/shard_map/all_to_all | solution.py:57
  70.6 1.5 reshape_reshape.6
  72.1 14.2 %all-to-all-done.1 = f32[16,1,16384]{2,1,0:T(1,128)S(1)} async-done(((f32[16,1,16384]{2,1,0:T(1,128)}), f32[16,1,16384]{2,1,0:T(1,128)S(1)}, u32[]{:S(2)}, u32[]{:S(2)}) %all-to-all-start.1) | async-done | bytes 1048608 | tf_op jit(solution)/shard_map/all_to_all | solution.py:54
  86.3 0.5 broadcast.42
  86.8 4.3 %reduce = f32[16,16384]{1,0:T(8,128)} reduce(f32[16,1,16384]{2,1,0:T(1,128)S(1)} %all-to-all-done.1, f32[]{:T(128)} %broadcast.42), dimensions={1}, to_apply=%all_to_all.30.reduce_sub_computation | reduce | bytes 2097156 | tf_op jit(solution)/shard_map/all_to_all | solution.py:54
  91.1 2.1 reshape.17
  93.2 1.5 copy.23
  94.7 2.3 %reshape_reshape.7 = f32[2,128,1024]{2,1,0:T(8,128)S(1)} reshape(f32[2,16,8,16,64]{4,3,2,1,0:T(8,128)} %copy.23) | data formatting | bytes 2097152 | tf_op jit(solution)/shard_map/reshape;reshape | solution.py:59
  97.0 1.1 convolution_convert_fusion
  98.1 2.7 %fusion.35 = f32[1024,1024]{0,1:T(8,128)} fusion(bf16[1024,256]{1,0:T(8,128)(2,1)S(1)} %copy-done, bf16[256,1024]{1,0:T(8,128)(2,1)S(1)} %bitcast.126), kind=kOutput, calls=%fused_computation.70 | convolution fusion | flops 536870912 | bytes 5242880 | tf_op jit(solution)/shard_map/dot_general | solution.py:36
  100.7 4.6 %fusion.7 = f32[256,1024]{1,0:T(8,128)S(1)} fusion(bf16[1024,256]{1,0:T(8,128)(2,1)S(1)} %copy-done, f32[1024,1024]{0,1:T(8,128)} %fusion.35, bf16[256,1024]{1,0:T(8,128)(2,1)} %param.11, bf16[256,1024]{1,0:T(8,128)(2,1)S(1)} %copy-done.3), kind=kOutput, calls=%fused_computation.16 | convolution fusion | flops 1083703296 | bytes 6815744 | tf_op jit(solution)/shard_map/dot_general | solution.py:43
  105.3 2.8 %fusion.34 = f32[2,1024,128]{2,1,0:T(8,128)} fusion(f32[2,128,1024]{2,1,0:T(8,128)S(1)} %bitcast.127, f32[2,128,128]{2,1,0:T(8,128)S(1)} %copy-done.4), kind=kOutput, calls=%fused_computation.69 | convolution fusion | flops 402653184 | bytes 2228224 | tf_op jit(solution)/shard_map/fkl,fkc->flc/dot_general | solution.py:47
  108.1 3.1 %copy.26 = f32[2,128,16,64]{3,2,0,1:T(8,128)S(1)} copy(f32[2,128,16,64]{1,3,2,0:T(8,128)} %bitcast.125) | data formatting | bytes 2097152 | tf_op jit(solution)/shard_map/reshape | solution.py:61
  111.2 2.3 %reshape.20 = f32[16,1,16384]{2,1,0:T(1,128)} reshape(f32[128,2,16,64]{3,2,1,0:T(8,128)S(1)} %bitcast.121) | data formatting | bytes 2097152
  113.4 32.0 %all_to_all.38 = f32[16,1,16384]{2,1,0:T(1,128)S(1)} all-to-all(f32[16,1,16384]{2,1,0:T(1,128)} %reshape.20), channel_id=1, replica_groups=mesh['lev'=16,'hor'=32] {'lev'}, dimensions={0} | all-to-all | bytes 2097152 | tf_op jit(solution)/shard_map/all_to_all | solution.py:64
  145.4 4.3 %reduce.1 = f32[16,16384]{1,0:T(8,128)} reduce(f32[16,1,16384]{2,1,0:T(1,128)S(1)} %all_to_all.38, f32[]{:T(128)} %broadcast.42), dimensions={1}, to_apply=%all_to_all.31.reduce_sub_computation | reduce | bytes 2097156 | tf_op jit(solution)/shard_map/all_to_all | solution.py:64
  149.7 2.1 reshape.21
  151.8 2.6 %copy.28 = f32[2,8,16,16,64]{4,3,2,1,0:T(8,128)} copy(f32[2,8,16,16,64]{4,2,0,1,3:T(8,128)S(1)} %bitcast.123) | data formatting | bytes 2097152 | tf_op jit(solution)/shard_map/all_to_all | solution.py:64
  154.3 2.0 all_to_all.34
  156.3 0.1 broadcast_multiply_fusion
  156.4 0.1 fusion.32
  156.5 43.8 %collective-permute-start.3 = (f32[2,8,1,1024]{3,2,1,0:T(1,128)S(1)}, f32[2,8,1,1024]{3,2,1,0:T(1,128)S(1)}, u32[]{:S(2)}, u32[]{:S(2)}) collective-permute-start(f32[2,8,1,1024]{3,2,1,0:T(1,128)S(1)} %get-tuple-element.5), channel_id=1, source_target_pairs={{0,1},{1,2},{2,3},{3,4},{4,5},{5,6},{6,7},{7,8},{8,9},{9,10},{10,1... | collective-permute-start | bytes 196616 | tf_op jit(solution)/shard_map/ppermute | solution.py:12
  200.4 1.9 collective-permute-start.2
  202.3 0.0 collective-permute-done.3
  202.3 6.3 %collective-permute-done.2 = f32[2,8,1,1024]{3,2,1,0:T(1,128)S(1)} collective-permute-done((f32[2,8,1,1024]{3,2,1,0:T(1,128)S(1)}, f32[2,8,1,1024]{3,2,1,0:T(1,128)S(1)}, u32[]{:S(2)}, u32[]{:S(2)}) %collective-permute-start.2) | collective-permute-done | bytes 65568 | tf_op jit(solution)/shard_map/ppermute | solution.py:15
  208.7 0.9 select_maximum_fusion
  209.6 1.7 fusion.9
  (19 shorter events, 0.2 us)
Async XLA Ops:
  0.0 98.0 %copy-start = (bf16[1024,256]{1,0:T(8,128)(2,1)S(1)}, bf16[1024,256]{1,0:T(8,128)(2,1)}, u32[]{:S(2)}) copy-start(bf16[1024,256]{1,0:T(8,128)(2,1)} %param.10) | copy-start | bytes 1572868
  1.4 35.9 %collective-permute-start.1 = (f32[2,8,1,1024]{3,2,1,0:T(1,128)S(1)}, f32[2,8,1,1024]{3,2,1,0:T(1,128)S(1)}, u32[]{:S(2)}, u32[]{:S(2)}) collective-permute-start(f32[2,8,1,1024]{3,2,1,0:T(1,128)S(1)} %get-tuple-element.7), channel_id=1, source_target_pairs={{0,1},{1,2},{2,3},{3,4},{4,5},{5,6},{6,7},{7,8},{8,9},{9,10},{10,1... | collective-permute-start | bytes 196616 | tf_op jit(solution)/shard_map/ppermute | solution.py:12
  4.9 32.4 %collective-permute-start = (f32[2,8,1,1024]{3,2,1,0:T(1,128)S(1)}, f32[2,8,1,1024]{3,2,1,0:T(1,128)S(1)}, u32[]{:S(2)}, u32[]{:S(2)}) collective-permute-start(f32[2,8,1,1024]{3,2,1,0:T(1,128)S(1)} %get-tuple-element.8), channel_id=1, source_target_pairs={{1,0},{2,1},{3,2},{4,3},{5,4},{6,5},{7,6},{8,7},{9,8},{10,9},{11,1... | collective-permute-start | bytes 196616 | tf_op jit(solution)/shard_map/ppermute | solution.py:15
  12.9 24.4 %copy-start.1 = (f32[2,8,16,1024]{3,2,1,0:T(8,128)S(1)}, f32[2,8,16,1024]{3,2,1,0:T(8,128)}, u32[]{:S(2)}) copy-start(f32[2,8,16,1024]{3,2,1,0:T(8,128)} %param.6) | copy-start | bytes 3145732
  19.4 18.8 %copy-start.2 = (f32[8,16,1024]{2,1,0:T(8,128)S(1)}, f32[8,16,1024]{2,1,0:T(8,128)}, u32[]{:S(2)}) copy-start(f32[8,16,1024]{2,1,0:T(8,128)} %param.8) | copy-start | bytes 1572868
  19.4 37.9 %all-to-all-start = ((bf16[16,2,8192]{2,1,0:T(2,128)(2,1)}), bf16[16,2,8192]{2,1,0:T(2,128)(2,1)}, u32[]{:S(2)}, u32[]{:S(2)}) async-start(bf16[16,2,8192]{2,1,0:T(2,128)(2,1)} %reshape.18), calls=%async_computation | async-start | bytes 1048576 | tf_op jit(solution)/shard_map/all_to_all | solution.py:57
  57.4 29.0 %all-to-all-start.1 = ((f32[16,1,16384]{2,1,0:T(1,128)}), f32[16,1,16384]{2,1,0:T(1,128)S(1)}, u32[]{:S(2)}, u32[]{:S(2)}) async-start(f32[16,1,16384]{2,1,0:T(1,128)} %reshape.16), calls=%async_computation.1 | async-start | bytes 2097152 | tf_op jit(solution)/shard_map/all_to_all | solution.py:54
  94.7 2.3 %copy-start.4 = (f32[2,128,128]{2,1,0:T(8,128)S(1)}, f32[2,128,128]{2,1,0:T(8,128)}, u32[]{:S(2)}) copy-start(f32[2,128,128]{2,1,0:T(8,128)} %param.9) | copy-start | bytes 393220
  98.0 2.7 %copy-start.3 = (bf16[256,1024]{1,0:T(8,128)(2,1)S(1)}, bf16[256,1024]{1,0:T(8,128)(2,1)}, u32[]{:S(2)}) copy-start(bf16[256,1024]{1,0:T(8,128)(2,1)} %reshape_reshape.6) | copy-start | bytes 1572868
  156.5 45.8 %collective-permute-start.3 = (f32[2,8,1,1024]{3,2,1,0:T(1,128)S(1)}, f32[2,8,1,1024]{3,2,1,0:T(1,128)S(1)}, u32[]{:S(2)}, u32[]{:S(2)}) collective-permute-start(f32[2,8,1,1024]{3,2,1,0:T(1,128)S(1)} %get-tuple-element.5), channel_id=1, source_target_pairs={{0,1},{1,2},{2,3},{3,4},{4,5},{5,6},{6,7},{7,8},{8,9},{9,10},{10,1... | collective-permute-start | bytes 196616 | tf_op jit(solution)/shard_map/ppermute | solution.py:12
  200.4 8.3 %collective-permute-start.2 = (f32[2,8,1,1024]{3,2,1,0:T(1,128)S(1)}, f32[2,8,1,1024]{3,2,1,0:T(1,128)S(1)}, u32[]{:S(2)}, u32[]{:S(2)}) collective-permute-start(f32[2,8,1,1024]{3,2,1,0:T(1,128)S(1)} %get-tuple-element.6), channel_id=1, source_target_pairs={{1,0},{2,1},{3,2},{4,3},{5,4},{6,5},{7,6},{8,7},{9,8},{10,9},{11,1... | collective-permute-start | bytes 196616 | tf_op jit(solution)/shard_map/ppermute | solution.py:15
